TPU v7x, 32 devices: a whole 2x2x4 slice. The times are simulated.
32 devices in a mesh: cam: 16 (over z, y, core), frame: 2 (over x).
Axes of the slice: x: 2, y: 2, z: 4, core: 2. Of those that a mesh axis runs over, the one named last changes fastest.
Arguments:
- frames: bfloat16 [16, 64, 3, 4096], P('cam', 'frame'), may hold values from -6 to 6
- conv1_w: bfloat16 [27, 128], replicated, may hold values from -1.25 to 1.25
- conv2_w: bfloat16 [1152, 256], replicated, may hold values from -0.1875 to 0.1875
- tile_w: bfloat16 [256, 128], replicated, may hold values from -0.375 to 0.375
- vis_subject: int32 [16, 64, 12], P('cam', 'frame'), may hold values from 0 to 63, as said below
- part_count: int32 [16, 64, 12], P('cam', 'frame'), may hold values from 6 to 8
- part_region: int32 [16, 64, 12, 8], P('cam', 'frame'), may hold values from 0 to 15
- subject_slot: int32 [64], replicated, may hold values from 0 to 63, as said below
- qkv_w: bfloat16 [1024, 3072], replicated, may hold values from -0.1875 to 0.1875
- out_w: bfloat16 [1024, 1024], replicated, may hold values from -0.1875 to 0.1875
- key_bias: float32 [64, 16, 64], P('cam'), may hold values from -2 to 237
Outputs:
- posed: bfloat16 [64, 64, 1024], P('cam', 'frame')
Inputs may be any that keep to these rules, and one draw needn't show every extreme that they name: `vis_subject`: each camera frame lists 12 distinct subjects. Rows of the subject-owned arrays form blocks of 4 (the rows of one index of cam); one list names at most 2 subjects whose rows lie in one block, and for each aligned block of 32 frames one row block, drawn for it, has exactly 2 subjects in every camera's list of every frame of it. `subject_slot`: A permutation of the subjects' numbers.
All inputs are finite; a program needn't handle non-finite values.
Results may differ from a plain program's by a relative error of at most 0.0085.
Values may be sent and summed in bfloat16 or wider, within the bound.
No kernel may reach another device: no remote copies, remote signals or barrier semaphores. Data moves between devices by JAX's collectives and lax.ppermute only.
A program may use at most 64 MiB of HBM per device.

v0:
```python
import math
import jax
import jax.numpy as jnp
from jax import lax
from jax.sharding import PartitionSpec as P

IMG = 64
RGRID = 4
C1 = 128
C2 = 256
TILE = 128
HEADS = 16
SUBJ_DEV = 4
PER_OWN = 2
EPS = 1e-05
NEG_START = -1e30


def conv_features(pictures, conv1_w, conv2_w):
    amount = pictures.shape[0]
    images = pictures.reshape(amount, 3, IMG, IMG)
    section_one = lax.conv_general_dilated(
        images,
        conv1_w.reshape(3, 3, 3, C1),
        (2, 2),
        ((1, 1), (1, 1)),
        dimension_numbers=("NCHW", "HWIO", "NHWC"),
        preferred_element_type=jnp.float32,
    )
    section_one = jax.nn.relu(section_one).astype(jnp.bfloat16)
    section_two = lax.conv_general_dilated(
        section_one,
        conv2_w.reshape(3, 3, C1, C2),
        (2, 2),
        ((1, 1), (1, 1)),
        dimension_numbers=("NHWC", "HWIO", "NHWC"),
        preferred_element_type=jnp.float32,
    )
    section_two = jax.nn.relu(section_two)
    patch_side = IMG // (4 * RGRID)
    pooled = jnp.mean(
        section_two.reshape(amount, RGRID, patch_side, RGRID, patch_side, C2), axis=(2, 4)
    )
    return pooled.reshape(amount, RGRID * RGRID, C2).astype(jnp.bfloat16)


def select_parts(features, part_region, part_count):
    frames_here, listed, part_total = part_region.shape
    regions = features.shape[1]
    visible = jnp.arange(part_total, dtype=jnp.int32)[None, None, :] < part_count[:, :, None]
    chooser = (part_region[:, :, :, None] == jnp.arange(regions, dtype=jnp.int32)) & visible[
        :, :, :, None
    ]
    chooser = chooser.astype(jnp.bfloat16).reshape(frames_here, listed * part_total, regions)
    picked = jnp.einsum("fer,frc->fec", chooser, features, preferred_element_type=jnp.float32)
    return picked.astype(jnp.bfloat16).reshape(frames_here * listed, part_total * features.shape[2])


def build_buffers(payload, vis_subject, subject_slot, owners, frames_here):
    listed = vis_subject.shape[1]
    entries = frames_here * listed
    subjects = subject_slot.shape[0]
    flat_ids = vis_subject.reshape(entries)
    slot_rows = jnp.sum(
        jnp.where(
            flat_ids[:, None] == jnp.arange(subjects, dtype=jnp.int32), subject_slot[None, :], 0
        ),
        axis=1,
    )
    owner_index = slot_rows // SUBJ_DEV
    member = (owner_index[:, None] == jnp.arange(owners, dtype=jnp.int32)).astype(jnp.int32)
    arrival = jnp.sum((jnp.cumsum(member, axis=0) - 1) * member, axis=1)
    capacity = PER_OWN * frames_here
    target = owner_index * capacity + arrival
    source = (
        jnp.full((owners * capacity,), entries, jnp.int32)
        .at[target]
        .set(jnp.arange(entries, dtype=jnp.int32))
    )
    padded = jnp.concatenate([payload, jnp.zeros((1, payload.shape[1]), payload.dtype)], axis=0)
    frame_of = jnp.arange(entries, dtype=jnp.int32) // listed
    placement_code = slot_rows % SUBJ_DEV * frames_here + frame_of
    codes = jnp.concatenate([placement_code, jnp.full((1,), SUBJ_DEV * frames_here, jnp.int32)])
    outgoing = padded[source].reshape(owners, capacity, payload.shape[1])
    return (outgoing, codes[source].reshape(owners, capacity))


def collect_tokens(received, arrived, rows):
    flat_rows = received.reshape(-1, received.shape[2])
    picker = (jnp.arange(rows, dtype=jnp.int32)[:, None] == arrived.reshape(1, -1)).astype(
        jnp.bfloat16
    )
    return jnp.dot(picker, flat_rows, preferred_element_type=jnp.float32)


def per_device(
    frames,
    conv1_w,
    conv2_w,
    tile_w,
    vis_subject,
    part_count,
    part_region,
    subject_slot,
    qkv_w,
    out_w,
    key_bias,
):
    pictures = frames[0]
    frames_here = pictures.shape[0]
    owners = lax.axis_size("cam")
    pooled = conv_features(pictures, conv1_w, conv2_w)
    projected = jnp.dot(pooled.reshape(-1, C2), tile_w, preferred_element_type=jnp.float32)
    tiles = projected.astype(jnp.bfloat16).reshape(frames_here, -1, TILE)
    payload = select_parts(tiles, part_region[0], part_count[0])
    outgoing, codes = build_buffers(payload, vis_subject[0], subject_slot, owners, frames_here)
    received, arrived = (
        lax.all_to_all(outgoing, "cam", split_axis=0, concat_axis=0, tiled=True),
        lax.all_to_all(codes, "cam", split_axis=0, concat_axis=0, tiled=True),
    )
    tokens = collect_tokens(received, arrived, SUBJ_DEV * frames_here)
    width = tokens.shape[1]
    head_size = width // HEADS
    score_scale = 1.0 / math.sqrt(head_size)
    normed = (tokens * lax.rsqrt(jnp.mean(tokens * tokens, axis=1, keepdims=True) + EPS)).astype(
        jnp.bfloat16
    )
    mixed = jnp.dot(normed, qkv_w, preferred_element_type=jnp.float32).astype(jnp.bfloat16)
    queries = mixed[:, :width].reshape(SUBJ_DEV, frames_here, HEADS, head_size)
    key_rows = mixed[:, width : 2 * width].reshape(SUBJ_DEV, frames_here, width)
    value_rows = mixed[:, 2 * width :].reshape(SUBJ_DEV, frames_here, width)
    row_top = jnp.full((SUBJ_DEV, HEADS, frames_here), NEG_START, jnp.float32)
    key_piece = lax.all_gather(key_rows, "frame", axis=1, tiled=True)
    value_piece = lax.all_gather(value_rows, "frame", axis=1, tiled=True)
    span = key_piece.shape[1]
    scores = (
        jnp.einsum(
            "sqhd,skhd->shqk",
            queries,
            key_piece.reshape(SUBJ_DEV, span, HEADS, head_size),
            preferred_element_type=jnp.float32,
        )
        * score_scale
    )
    scores = scores + key_bias[:, :, None, :]
    new_top = jnp.maximum(row_top, jnp.max(scores, axis=3))
    weights = jnp.exp(scores - new_top[..., None])
    denominator = jnp.sum(weights, axis=3)
    numerator = jnp.einsum(
        "shqk,skhd->shqd",
        weights.astype(jnp.bfloat16),
        value_piece.reshape(SUBJ_DEV, span, HEADS, head_size),
        preferred_element_type=jnp.float32,
    )
    row_top, denominator, numerator = (new_top, denominator, numerator)
    attended = numerator / denominator[..., None]
    attended = (
        jnp.transpose(attended, (0, 2, 1, 3))
        .reshape(SUBJ_DEV * frames_here, width)
        .astype(jnp.bfloat16)
    )
    posed = tokens + jnp.dot(attended, out_w, preferred_element_type=jnp.float32)
    return posed.astype(jnp.bfloat16).reshape(SUBJ_DEV, frames_here, width)


def solution(mesh):
    in_specs = (
        P("cam", "frame", None, None),
        P(),
        P(),
        P(),
        P("cam", "frame", None),
        P("cam", "frame", None),
        P("cam", "frame", None, None),
        P(),
        P(),
        P(),
        P("cam", None, None),
    )
    out_specs = P("cam", "frame", None)
    return jax.shard_map(
        per_device, mesh=mesh, in_specs=in_specs, out_specs=out_specs, check_vma=False
    )
```

profile of v0, /device:TPU:12, one launch (start us, length us, event | category | flops | bytes accessed | tf_op | source)
XLA Modules:
  0.0 141.6 jit_solution(5429485537469918314)
XLA Ops:
  0.0 0.0 copy-start
  0.0 0.0 copy-start.1
  0.0 0.9 copy.44
  0.9 0.1 eq.70
  1.0 0.8 select_reduce_fusion
  1.8 0.9 reduce-window.6
  2.7 0.2 slice_reduce_fusion
  3.0 0.1 fusion.21
  3.1 2.9 %scatter_custom_fusion = s32[1024]{0:T(1024)S(1)} fusion(s32[384]{0:T(512)S(1)} %fusion.35, s32[384]{0:T(512)S(1)} %iota.33, s32[]{:T(128)} %constant.64.clone.1), kind=kCustom, calls=%fused_computation.78 | custom fusion | bytes 4100 | tf_op jit(solution)/shard_map/scatter | solution.py:78
  6.1 0.0 copy-start.5
  6.1 0.0 copy-start.7
  6.1 6.9 %gather_fusion = s32[1024]{0:T(1024)S(1)} fusion(s32[385]{0:T(512)S(1)} %pad_add_fusion, s32[1024]{0:T(1024)S(1)} %fusion.23), kind=kCustom, calls=%fused_computation | custom fusion | bytes 12288 | tf_op jit(solution)/shard_map/gather | solution.py:85
  13.0 0.7 all_to_all.9
  13.6 6.2 %all-to-all-start = ((s32[16,1,64]{2,1,0:T(1,128)}), s32[16,1,64]{2,1,0:T(1,128)S(1)}, u32[]{:S(2)}, u32[]{:S(2)}) async-start(s32[16,1,64]{2,1,0:T(1,128)} %all_to_all.9), calls=%async_computation | async-start | bytes 16384 | tf_op jit(solution)/shard_map/all_to_all | solution.py:119
  19.9 0.0 copy-done.1
  19.9 4.7 %copy.54 = bf16[1,32,3,4096]{1,2,3,0:T(4,128)(2,1)} copy(bf16[1,32,3,4096]{3,1,2,0:T(8,128)(2,1)S(1)} %copy-done.1) | data formatting | bytes 1572864 | tf_op jit(solution)/shard_map/reshape;squeeze | solution.py:21
  24.6 0.0 copy-done.5
  24.6 0.0 copy-done.7
  24.6 15.4 %broadcast_maximum_fusion = f32[32,16,16,256]{3,0,2,1:T(8,128)} fusion(bf16[3,3,128,256]{3,2,1,0:T(8,128)(2,1)S(1)} %bitcast.76, bf16[32,3,64,64]{0,1,3,2:T(4,128)(2,1)} %bitcast.68, bf16[3,3,3,128]{3,2,1,0:T(4,128)(2,1)S(1)} %reshape.171), kind=kOutput, calls=%fused_computation.6 | convolution fusion | flops 4864892928 | bytes 9771776 | tf_op jit(solution)/shard_map/conv_general_dilated | solution.py:31
  40.0 0.0 copy-start.3
  40.0 0.0 copy-start.6
  40.0 0.0 copy-start.2
  40.0 4.4 %reduce_sum.56 = f32[32,4,4,256]{3,0,2,1:T(8,128)S(1)} reduce(f32[32,4,4,4,4,256]{5,0,4,3,2,1:T(8,128)} %bitcast.67, f32[]{:T(128)} %constant.69.clone.1), dimensions={2,4}, to_apply=%region_5.6 | reduce | flops 1966080 | bytes 8912900 | tf_op jit(solution)/shard_map/reduce_sum | solution.py:41
  44.5 0.2 copy.49
  44.7 0.1 convert_element_type.44
  44.8 0.0 copy-done.3
  44.8 0.1 copy.46
  44.9 0.0 copy-done.6
  44.9 0.1 lt.50
  45.0 0.1 bitcast_compare_fusion
  45.1 0.1 copy.47
  45.1 0.0 copy-done.2
  45.1 0.2 convolution_convert_fusion.2
  45.4 0.6 convolution_convert_fusion.1
  46.0 1.2 reshape.175
  47.2 1.2 concatenate.7
  48.4 5.4 %gather_fusion.1 = bf16[1024,1024]{1,0:T(8,128)(2,1)} fusion(bf16[385,1024]{1,0:T(8,128)(2,1)S(1)} %concatenate.7, s32[1024]{0:T(1024)S(1)} %fusion.23), kind=kCustom, calls=%fused_computation.1 | custom fusion | bytes 4198400 | tf_op jit(solution)/shard_map/gather | solution.py:84
  53.8 0.0 all-to-all-done
  53.8 6.0 %all-to-all-start.1 = ((bf16[16,64,1024]{2,1,0:T(8,128)(2,1)}), bf16[16,64,1024]{2,1,0:T(8,128)(2,1)}, u32[]{:S(2)}, u32[]{:S(2)}) async-start(bf16[16,64,1024]{2,1,0:T(8,128)(2,1)} %bitcast.66), calls=%async_computation.1 | async-start | bytes 4194304 | tf_op jit(solution)/shard_map/all_to_all | solution.py:118
  59.8 0.5 broadcast.219
  60.3 0.7 reduce.7
  61.0 0.1 eq.80
  61.1 46.0 %all-to-all-done.1 = bf16[16,64,1024]{2,1,0:T(8,128)(2,1)} async-done(((bf16[16,64,1024]{2,1,0:T(8,128)(2,1)}), bf16[16,64,1024]{2,1,0:T(8,128)(2,1)}, u32[]{:S(2)}, u32[]{:S(2)}) %all-to-all-start.1) | async-done | bytes 2097184 | tf_op jit(solution)/shard_map/all_to_all | solution.py:118
  107.0 2.1 %multiply_reduce_fusion = (f32[128]{0:T(128)S(1)}, f32[128,1024]{1,0:T(8,128)S(1)}) fusion(bf16[1024,1024]{1,0:T(8,128)(2,1)} %bitcast.9, s32[1024]{0:T(1024)S(1)} %eq.80), kind=kOutput, calls=%fused_computation.25 | convolution fusion | flops 268828544 | bytes 2626048 | tf_op jit(solution)/shard_map/dot_general | solution.py:93
  109.2 3.8 %convolution_convert_fusion = bf16[128,3072]{1,0:T(8,128)(2,1)S(1)} fusion(bf16[1024,3072]{1,0:T(8,128)(2,1)} %param.19, f32[128,1024]{1,0:T(8,128)S(1)} %get-tuple-element.11, f32[128]{0:T(128)S(1)} %add_rsqrt_fusion), kind=kOutput, calls=%fused_computation.7 | convolution fusion | flops 805961728 | bytes 7602688 | tf_op jit(solution)/shard_map/dot_general | solution.py:128
  113.0 0.0 copy-start.4
  113.0 0.8 fusion.37
  113.8 9.3 %all_gather.7 = bf16[4,64,1024]{2,1,0:T(8,128)(2,1)S(1)} all-gather(bf16[4,32,1024]{2,1,0:T(8,128)(2,1)S(1)} %bitcast.70), channel_id=1, replica_groups=mesh['cam'=16,'frame'=2] {'frame'}, dimensions={1}, use_global_device_ids=true | all-gather | bytes 786432 | tf_op jit(solution)/shard_map/all_gather | solution.py:134
  123.0 1.7 %reshape.182 = bf16[4,64,16,64]{3,2,1,0:T(8,128)(2,1)} reshape(bf16[4,64,1024]{2,1,0:T(8,128)(2,1)S(1)} %all_gather.7) | data formatting | bytes 1048576 | tf_op jit(solution)/shard_map/reshape | solution.py:152
  124.7 8.6 %all_gather.6 = bf16[4,64,1024]{2,1,0:T(8,128)(2,1)S(1)} all-gather(bf16[4,32,1024]{2,1,0:T(8,128)(2,1)} %bitcast.69), channel_id=1, replica_groups=mesh['cam'=16,'frame'=2] {'frame'}, dimensions={1}, use_global_device_ids=true | all-gather | bytes 786432 | tf_op jit(solution)/shard_map/all_gather | solution.py:133
  133.3 1.7 %reshape.180 = bf16[4,64,16,64]{3,2,1,0:T(8,128)(2,1)} reshape(bf16[4,64,1024]{2,1,0:T(8,128)(2,1)S(1)} %all_gather.6) | data formatting | bytes 1048576 | tf_op jit(solution)/shard_map/reshape | solution.py:140
  135.0 0.3 reshape.178
  135.3 0.0 copy-done.4
  135.3 2.0 %fusion.38 = (f32[4,16,32]{2,1,0:T(8,128)S(1)}, f32[4,16,32,64]{3,2,1,0:T(8,128)S(1)}) fusion(f32[4,16,64]{2,1,0:T(8,128)S(1)} %copy-done.4, bf16[4,64,16,64]{3,2,1,0:T(8,128)(2,1)} %reshape.180, bf16[4,32,16,64]{3,2,1,0:T(8,128)(2,1)S(1)} %reshape.178), kind=kOutput, calls=%fused_computation.88 | convolution fusion | flops 17168384 | bytes 1335296 | tf_op jit(solution)/shard_map/sqhd,skhd->shqk/dot_general | solution.py:137
  137.3 0.6 fusion.8
  138.0 1.9 %fusion.4 = bf16[4,32,16,64]{3,1,2,0:T(8,128)(2,1)S(1)} fusion(bf16[4,64,16,64]{3,2,1,0:T(8,128)(2,1)} %reshape.182, f32[4,16,32,64]{3,2,1,0:T(8,128)S(1)} %get-tuple-element.13, f32[4,32,16]{1,2,0:T(8,128)S(1)} %bitcast.73, f32[4,16,32]{2,1,0:T(8,128)S(1)} %broadcast_maximum_fusion.1), kind=kOutput, calls=%fused_computation.13 | convolution fusion | flops 17301504 | bytes 1327104 | tf_op jit(solution)/shard_map/shqk,skhd->shqd/dot_general | solution.py:149
  139.8 0.2 copy.53
  140.0 0.3 convert_element_type.51
  140.4 0.0 copy-done
  140.4 1.2 fusion.5
  (14 shorter events, 0.2 us)
Async XLA Ops:
  0.0 140.4 %copy-start = (bf16[1024,1024]{1,0:T(8,128)(2,1)S(1)}, bf16[1024,1024]{1,0:T(8,128)(2,1)}, u32[]{:S(2)}) copy-start(bf16[1024,1024]{1,0:T(8,128)(2,1)} %param.20) | copy-start | bytes 6291460
  0.0 19.9 %copy-start.1 = (bf16[1,32,3,4096]{3,1,2,0:T(8,128)(2,1)S(1)}, bf16[1,32,3,4096]{3,1,2,0:T(8,128)(2,1)}, u32[]{:S(2)}) copy-start(bf16[1,32,3,4096]{3,1,2,0:T(8,128)(2,1)} %param.11) | copy-start | bytes 2359300
  6.1 18.6 %copy-start.5 = (bf16[27,128]{1,0:T(8,128)(2,1)S(1)}, bf16[27,128]{1,0:T(8,128)(2,1)}, u32[]{:S(2)}) copy-start(bf16[27,128]{1,0:T(8,128)(2,1)} %param.12) | copy-start | bytes 20740
  6.1 18.6 %copy-start.7 = (bf16[1152,256]{1,0:T(8,128)(2,1)S(1)}, bf16[1152,256]{1,0:T(8,128)(2,1)}, u32[]{:S(2)}) copy-start(bf16[1152,256]{1,0:T(8,128)(2,1)} %param.13) | copy-start | bytes 1769476
  13.6 40.1 %all-to-all-start = ((s32[16,1,64]{2,1,0:T(1,128)}), s32[16,1,64]{2,1,0:T(1,128)S(1)}, u32[]{:S(2)}, u32[]{:S(2)}) async-start(s32[16,1,64]{2,1,0:T(1,128)} %all_to_all.9), calls=%async_computation | async-start | bytes 16384 | tf_op jit(solution)/shard_map/all_to_all | solution.py:119
  40.0 4.8 %copy-start.3 = (s32[1,32,12,8]{1,3,2,0:T(8,128)S(1)}, s32[1,32,12,8]{1,3,2,0:T(8,128)}, u32[]{:S(2)}) copy-start(s32[1,32,12,8]{1,3,2,0:T(8,128)} %param.17) | copy-start | bytes 36868
  40.0 4.8 %copy-start.6 = (s32[1,32,12]{1,0,2:T(1,128)S(1)}, s32[1,32,12]{1,0,2:T(1,128)}, u32[]{:S(2)}) copy-start(s32[1,32,12]{1,0,2:T(1,128)} %param.16) | copy-start | bytes 4612
  40.0 5.1 %copy-start.2 = (bf16[256,128]{1,0:T(8,128)(2,1)S(1)}, bf16[256,128]{1,0:T(8,128)(2,1)}, u32[]{:S(2)}) copy-start(bf16[256,128]{1,0:T(8,128)(2,1)} %param.14) | copy-start | bytes 196612
  53.8 53.3 %all-to-all-start.1 = ((bf16[16,64,1024]{2,1,0:T(8,128)(2,1)}), bf16[16,64,1024]{2,1,0:T(8,128)(2,1)}, u32[]{:S(2)}, u32[]{:S(2)}) async-start(bf16[16,64,1024]{2,1,0:T(8,128)(2,1)} %bitcast.66), calls=%async_computation.1 | async-start | bytes 4194304 | tf_op jit(solution)/shard_map/all_to_all | solution.py:118
  113.0 22.3 %copy-start.4 = (f32[4,16,64]{2,1,0:T(8,128)S(1)}, f32[4,16,64]{2,1,0:T(8,128)}, u32[]{:S(2)}) copy-start(f32[4,16,64]{2,1,0:T(8,128)} %param.21) | copy-start | bytes 49156
where the time goes:
time: 142 us
  waiting for transfers between devices  46 us (32%)
  local copies, waits for them, and re-layouts  30.4 us (21%)
  matrix products  27.1 us (19%)
  blocking collectives  17.9 us (13%)
  starting transfers between devices  12.3 us (9%)
  other arithmetic  7.7 us (5%)
    all_to_all x1, waiting for transfers between devices, per_device(): lax.all_to_all(outgoing, 'cam', split_axis=0, concat_axis=0, tiled=True)  46 us
    conv_general_dilated x1, matrix products, conv_features(): lax.conv_general_dilated(section_one, conv2_w.reshape(3, 3, C1, C2), (2,...  15.4 us
    all_gather x1, blocking collectives, per_device(): value_piece = lax.all_gather(value_rows, 'frame', axis=1, tiled=True)  9.25 us
    all_gather x1, blocking collectives, per_device(): key_piece = lax.all_gather(key_rows, 'frame', axis=1, tiled=True)  8.6 us
    gather x1, local copies, waits for them, and re-layouts, build_buffers(): return (outgoing, codes[source].reshape(owners, capacity))  6.87 us
    all_to_all x1, starting transfers between devices, per_device(): lax.all_to_all(codes, 'cam', split_axis=0, concat_axis=0, tiled=True)  6.24 us
    all_to_all x1, starting transfers between devices, per_device(): lax.all_to_all(outgoing, 'cam', split_axis=0, concat_axis=0, tiled=True)  6.01 us
    gather x1, local copies, waits for them, and re-layouts, build_buffers(): outgoing = padded[source].reshape(owners, capacity, payload.shape[1])  5.39 us
  transfers between devices with their start and end apart: 2, of which 1 were waited for; matrix products, arithmetic and copies ran while one was open for 25% of the time, Pallas kernels for 0%

commit v1 on v0

--- a/solution.py
+++ b/solution.py
@@ -130,8 +130,13 @@
     key_rows = mixed[:, width : 2 * width].reshape(SUBJ_DEV, frames_here, width)
     value_rows = mixed[:, 2 * width :].reshape(SUBJ_DEV, frames_here, width)
     row_top = jnp.full((SUBJ_DEV, HEADS, frames_here), NEG_START, jnp.float32)
-    key_piece = lax.all_gather(key_rows, "frame", axis=1, tiled=True)
-    value_piece = lax.all_gather(value_rows, "frame", axis=1, tiled=True)
+    key_piece, value_piece = jnp.split(
+        jax.lax.all_gather(
+            jnp.concatenate([key_rows, value_rows], axis=0), "frame", axis=1, tiled=True
+        ),
+        [key_rows.shape[0]],
+        axis=0,
+    )
     span = key_piece.shape[1]
     scores = (
         jnp.einsum(

time: 142 us -> 164 us (1.15); the launches traced: 142 us -> 161 us
  waiting for transfers between devices: 46 us -> 66.2 us
  blocking collectives: 17.9 us -> 0 us
  between operations: 0.27 us -> 13.7 us
  local copies, waits for them, and re-layouts: 30.4 us -> 33.4 us
    all_gather x0 -> x1, waiting for transfers between devices: none -> 20.3 us  [per_device(): jax.lax.all_gather(jnp.concatenate([key_rows, value_rows], axis=0), 'fram...]
    all_gather x2 -> x0, blocking collectives: 17.9 us -> none  [the longest x1 9.25 us: per_device(): value_piece = lax.all_gather(value_rows, 'frame', axis=1, tiled=True)]
    split x0 -> x1, local copies, waits for them, and re-layouts: none -> 2.11 us  [per_device(): jnp.split(jax.lax.all_gather(jnp.concatenate([key_rows, value_rows], axis...]
  transfers between devices with their start and end apart: 2 -> 3, of which waited for: 1 -> 2; matrix products, arithmetic and copies ran while one was open for 25% -> 22% of each run, Pallas kernels for 0% -> 0%
where the time goes in v1:
time: 164 us; the launch traced here: 161 us
  waiting for transfers between devices  66.2 us (40%)
  local copies, waits for them, and re-layouts  33.4 us (20%)
  matrix products  27.3 us (17%)
  between operations  13.7 us (8%)
  starting transfers between devices  12.3 us (8%)
  other arithmetic  8.56 us (5%)
    all_to_all x1, waiting for transfers between devices, per_device(): lax.all_to_all(outgoing, 'cam', split_axis=0, concat_axis=0, tiled=True)  45.9 us
    all_gather x1, waiting for transfers between devices, per_device(): jax.lax.all_gather(jnp.concatenate([key_rows, value_rows], axis=0), 'fram...  20.3 us
    conv_general_dilated x1, matrix products, conv_features(): lax.conv_general_dilated(section_one, conv2_w.reshape(3, 3, C1, C2), (2,...  15.4 us
    gather x1, local copies, waits for them, and re-layouts, build_buffers(): return (outgoing, codes[source].reshape(owners, capacity))  6.87 us
    all_to_all x1, starting transfers between devices, per_device(): lax.all_to_all(codes, 'cam', split_axis=0, concat_axis=0, tiled=True)  6.24 us
    all_to_all x1, starting transfers between devices, per_device(): lax.all_to_all(outgoing, 'cam', split_axis=0, concat_axis=0, tiled=True)  6.01 us
    gather x1, local copies, waits for them, and re-layouts, build_buffers(): outgoing = padded[source].reshape(owners, capacity, payload.shape[1])  5.39 us
    another operation x1, local copies, waits for them, and re-layouts, conv_features(): images = pictures.reshape(amount, 3, IMG, IMG)  4.73 us
  transfers between devices with their start and end apart: 3, of which 2 were waited for; matrix products, arithmetic and copies ran while one was open for 22% of the time, Pallas kernels for 0%

profile of v1, /device:TPU:12, one launch (start us, length us, event | category | flops | bytes accessed | tf_op | source)
XLA Modules:
  0.0 161.4 jit_solution(3704364664102150055)
XLA Ops:
  6.5 0.0 copy-start
  6.5 0.0 copy-start.1
  6.5 0.9 copy.44
  7.5 0.1 eq.70
  7.6 0.8 select_reduce_fusion
  8.4 0.9 reduce-window.6
  9.2 0.2 slice_reduce_fusion
  9.5 0.1 fusion.21
  9.6 2.9 %scatter_custom_fusion = s32[1024]{0:T(1024)S(1)} fusion(s32[384]{0:T(512)S(1)} %fusion.35, s32[384]{0:T(512)S(1)} %iota.33, s32[]{:T(128)} %constant.64.clone.1), kind=kCustom, calls=%fused_computation.79 | custom fusion | bytes 4100 | tf_op jit(solution)/shard_map/scatter | solution.py:78
  12.6 0.0 copy-start.5
  12.6 0.0 copy-start.7
  12.6 6.9 %gather_fusion = s32[1024]{0:T(1024)S(1)} fusion(s32[385]{0:T(512)S(1)} %pad_add_fusion, s32[1024]{0:T(1024)S(1)} %fusion.23), kind=kCustom, calls=%fused_computation | custom fusion | bytes 12288 | tf_op jit(solution)/shard_map/gather | solution.py:85
  19.5 0.7 all_to_all.9
  20.2 6.2 %all-to-all-start = ((s32[16,1,64]{2,1,0:T(1,128)}), s32[16,1,64]{2,1,0:T(1,128)S(1)}, u32[]{:S(2)}, u32[]{:S(2)}) async-start(s32[16,1,64]{2,1,0:T(1,128)} %all_to_all.9), calls=%async_computation | async-start | bytes 16384 | tf_op jit(solution)/shard_map/all_to_all | solution.py:119
  26.4 0.0 copy-done.1
  26.4 4.7 %copy.54 = bf16[1,32,3,4096]{1,2,3,0:T(4,128)(2,1)} copy(bf16[1,32,3,4096]{3,1,2,0:T(8,128)(2,1)S(1)} %copy-done.1) | data formatting | bytes 1572864 | tf_op jit(solution)/shard_map/reshape;squeeze | solution.py:21
  31.1 0.0 copy-done.5
  31.2 0.0 copy-done.7
  31.2 15.4 %broadcast_maximum_fusion = f32[32,16,16,256]{3,0,2,1:T(8,128)} fusion(bf16[3,3,128,256]{3,2,1,0:T(8,128)(2,1)S(1)} %bitcast.76, bf16[32,3,64,64]{0,1,3,2:T(4,128)(2,1)} %bitcast.68, bf16[3,3,3,128]{3,2,1,0:T(4,128)(2,1)S(1)} %reshape.171), kind=kOutput, calls=%fused_computation.6 | convolution fusion | flops 4864892928 | bytes 9771776 | tf_op jit(solution)/shard_map/conv_general_dilated | solution.py:31
  46.6 0.0 copy-start.3
  46.6 0.0 copy-start.6
  46.6 0.0 copy-start.2
  46.6 4.4 %reduce_sum.56 = f32[32,4,4,256]{3,0,2,1:T(8,128)S(1)} reduce(f32[32,4,4,4,4,256]{5,0,4,3,2,1:T(8,128)} %bitcast.67, f32[]{:T(128)} %constant.69.clone.1), dimensions={2,4}, to_apply=%region_5.6 | reduce | flops 1966080 | bytes 8912900 | tf_op jit(solution)/shard_map/reduce_sum | solution.py:41
  51.0 0.2 copy.49
  51.2 0.1 convert_element_type.44
  51.3 0.0 copy-done.3
  51.3 0.1 copy.46
  51.4 0.0 copy-done.6
  51.4 0.1 lt.50
  51.5 0.1 bitcast_compare_fusion
  51.6 0.1 copy.47
  51.7 0.0 copy-done.2
  51.7 0.2 convolution_convert_fusion.2
  51.9 0.6 convolution_convert_fusion.1
  52.5 1.2 reshape.175
  53.7 1.2 concatenate.10
  54.9 5.4 %gather_fusion.1 = bf16[1024,1024]{1,0:T(8,128)(2,1)} fusion(bf16[385,1024]{1,0:T(8,128)(2,1)S(1)} %concatenate.10, s32[1024]{0:T(1024)S(1)} %fusion.23), kind=kCustom, calls=%fused_computation.1 | custom fusion | bytes 4198400 | tf_op jit(solution)/shard_map/gather | solution.py:84
  60.3 0.0 all-to-all-done
  60.3 6.0 %all-to-all-start.1 = ((bf16[16,64,1024]{2,1,0:T(8,128)(2,1)}), bf16[16,64,1024]{2,1,0:T(8,128)(2,1)}, u32[]{:S(2)}, u32[]{:S(2)}) async-start(bf16[16,64,1024]{2,1,0:T(8,128)(2,1)} %bitcast.66), calls=%async_computation.1 | async-start | bytes 4194304 | tf_op jit(solution)/shard_map/all_to_all | solution.py:118
  66.3 0.0 all-gather.2.cloned.1.call-start
  66.4 0.5 broadcast.219
  66.9 0.7 reduce.7
  67.6 0.1 eq.80
  67.6 45.9 %all-to-all-done.1 = bf16[16,64,1024]{2,1,0:T(8,128)(2,1)} async-done(((bf16[16,64,1024]{2,1,0:T(8,128)(2,1)}), bf16[16,64,1024]{2,1,0:T(8,128)(2,1)}, u32[]{:S(2)}, u32[]{:S(2)}) %all-to-all-start.1) | async-done | bytes 2097184 | tf_op jit(solution)/shard_map/all_to_all | solution.py:118
  113.6 2.1 %multiply_reduce_fusion = (f32[128]{0:T(128)S(1)}, f32[128,1024]{1,0:T(8,128)S(1)}) fusion(bf16[1024,1024]{1,0:T(8,128)(2,1)} %bitcast.9, s32[1024]{0:T(1024)S(1)} %eq.80), kind=kOutput, calls=%fused_computation.26 | convolution fusion | flops 268828544 | bytes 2626048 | tf_op jit(solution)/shard_map/dot_general | solution.py:93
  115.7 3.8 %convolution_convert_fusion = bf16[128,3072]{1,0:T(8,128)(2,1)S(1)} fusion(bf16[1024,3072]{1,0:T(8,128)(2,1)} %param.19, f32[128,1024]{1,0:T(8,128)S(1)} %get-tuple-element.13, f32[128]{0:T(128)S(1)} %add_rsqrt_fusion), kind=kOutput, calls=%fused_computation.7 | convolution fusion | flops 805961728 | bytes 7602688 | tf_op jit(solution)/shard_map/dot_general | solution.py:128
  119.5 0.1 fusion.38
  119.6 0.0 copy-start.4
  119.6 0.9 pad_maximum_fusion
  120.5 0.0 all-gather.2.cloned.1.call-update
  120.5 1.1 reshape.178
  121.6 20.3 %all-gather.2.cloned.1.call-done = bf16[8,64,1024]{2,1,0:T(8,128)(2,1)} async-done(((bf16[8,32,1024]{2,1,0:T(8,128)(2,1)}), bf16[8,64,1024]{2,1,0:T(8,128)(2,1)}) %all-gather.2.cloned.1.call-update) | async-done | bytes 1048592 | tf_op jit(solution)/shard_map/all_gather | solution.py:134
  141.9 2.1 %fusion.37 = (bf16[4,64,1024]{2,1,0:T(8,128)(2,1)S(1)}, bf16[4,64,1024]{2,1,0:T(8,128)(2,1)}) fusion(bf16[8,64,1024]{2,1,0:T(8,128)(2,1)} %all-gather.2.cloned.1.call-done), kind=kLoop, calls=%fused_computation.88 | loop fusion | bytes 2097152 | tf_op jit(solution)/shard_map/split | solution.py:133
  144.0 2.5 %reshape.182 = bf16[4,64,16,64]{3,2,1,0:T(8,128)(2,1)} reshape(bf16[4,64,1024]{2,1,0:T(8,128)(2,1)} %get-tuple-element.6) | data formatting | bytes 1048576 | tf_op jit(solution)/shard_map/reshape | solution.py:157
  146.5 1.7 %reshape.181 = bf16[4,64,16,64]{3,2,1,0:T(8,128)(2,1)} reshape(bf16[4,64,1024]{2,1,0:T(8,128)(2,1)S(1)} %get-tuple-element.5) | data formatting | bytes 1048576 | tf_op jit(solution)/shard_map/reshape | solution.py:145
  148.2 0.0 copy-done.4
  148.2 2.1 %fusion.39 = (f32[4,16,32]{2,1,0:T(8,128)S(1)}, f32[4,16,32,64]{3,2,1,0:T(8,128)S(1)}) fusion(f32[4,16,64]{2,1,0:T(8,128)S(1)} %copy-done.4, bf16[4,64,16,64]{3,2,1,0:T(8,128)(2,1)} %reshape.181, bf16[4,32,16,64]{3,2,1,0:T(8,128)(2,1)} %reshape.178), kind=kOutput, calls=%fused_computation.90 | convolution fusion | flops 17168384 | bytes 1335296 | tf_op jit(solution)/shard_map/sqhd,skhd->shqk/dot_general | solution.py:142
  150.3 0.6 fusion.8
  151.0 1.9 %fusion.4 = bf16[4,32,16,64]{3,1,2,0:T(8,128)(2,1)S(1)} fusion(bf16[4,64,16,64]{3,2,1,0:T(8,128)(2,1)} %reshape.182, f32[4,16,32,64]{3,2,1,0:T(8,128)S(1)} %get-tuple-element.15, f32[4,32,16]{1,2,0:T(8,128)S(1)} %bitcast.73, f32[4,16,32]{2,1,0:T(8,128)S(1)} %broadcast_maximum_fusion.1), kind=kOutput, calls=%fused_computation.13 | convolution fusion | flops 17301504 | bytes 1327104 | tf_op jit(solution)/shard_map/shqk,skhd->shqd/dot_general | solution.py:154
  152.9 0.2 copy.53
  153.1 0.3 convert_element_type.51
  153.4 0.0 copy-done
  153.4 1.2 fusion.5
  (14 shorter events, 0.2 us)
Async XLA Ops:
  6.5 146.9 %copy-start = (bf16[1024,1024]{1,0:T(8,128)(2,1)S(1)}, bf16[1024,1024]{1,0:T(8,128)(2,1)}, u32[]{:S(2)}) copy-start(bf16[1024,1024]{1,0:T(8,128)(2,1)} %param.20) | copy-start | bytes 6291460
  6.5 19.9 %copy-start.1 = (bf16[1,32,3,4096]{3,1,2,0:T(8,128)(2,1)S(1)}, bf16[1,32,3,4096]{3,1,2,0:T(8,128)(2,1)}, u32[]{:S(2)}) copy-start(bf16[1,32,3,4096]{3,1,2,0:T(8,128)(2,1)} %param.11) | copy-start | bytes 2359300
  12.6 18.6 %copy-start.5 = (bf16[27,128]{1,0:T(8,128)(2,1)S(1)}, bf16[27,128]{1,0:T(8,128)(2,1)}, u32[]{:S(2)}) copy-start(bf16[27,128]{1,0:T(8,128)(2,1)} %param.12) | copy-start | bytes 20740
  12.6 18.6 %copy-start.7 = (bf16[1152,256]{1,0:T(8,128)(2,1)S(1)}, bf16[1152,256]{1,0:T(8,128)(2,1)}, u32[]{:S(2)}) copy-start(bf16[1152,256]{1,0:T(8,128)(2,1)} %param.13) | copy-start | bytes 1769476
  20.2 40.1 %all-to-all-start = ((s32[16,1,64]{2,1,0:T(1,128)}), s32[16,1,64]{2,1,0:T(1,128)S(1)}, u32[]{:S(2)}, u32[]{:S(2)}) async-start(s32[16,1,64]{2,1,0:T(1,128)} %all_to_all.9), calls=%async_computation | async-start | bytes 16384 | tf_op jit(solution)/shard_map/all_to_all | solution.py:119
  46.6 4.8 %copy-start.3 = (s32[1,32,12,8]{1,3,2,0:T(8,128)S(1)}, s32[1,32,12,8]{1,3,2,0:T(8,128)}, u32[]{:S(2)}) copy-start(s32[1,32,12,8]{1,3,2,0:T(8,128)} %param.17) | copy-start | bytes 36868
  46.6 4.8 %copy-start.6 = (s32[1,32,12]{1,0,2:T(1,128)S(1)}, s32[1,32,12]{1,0,2:T(1,128)}, u32[]{:S(2)}) copy-start(s32[1,32,12]{1,0,2:T(1,128)} %param.16) | copy-start | bytes 4612
  46.6 5.1 %copy-start.2 = (bf16[256,128]{1,0:T(8,128)(2,1)S(1)}, bf16[256,128]{1,0:T(8,128)(2,1)}, u32[]{:S(2)}) copy-start(bf16[256,128]{1,0:T(8,128)(2,1)} %param.14) | copy-start | bytes 196612
  60.3 53.3 %all-to-all-start.1 = ((bf16[16,64,1024]{2,1,0:T(8,128)(2,1)}), bf16[16,64,1024]{2,1,0:T(8,128)(2,1)}, u32[]{:S(2)}, u32[]{:S(2)}) async-start(bf16[16,64,1024]{2,1,0:T(8,128)(2,1)} %bitcast.66), calls=%async_computation.1 | async-start | bytes 4194304 | tf_op jit(solution)/shard_map/all_to_all | solution.py:118
  66.3 75.6 %all-gather.2.cloned.1.call-start = ((), (), s32[]{:S(2)}) async-start(), calls=%async_computation.2 | async-start | bytes 1572864 | tf_op jit(solution)/shard_map/all_gather | solution.py:134
  119.6 28.6 %copy-start.4 = (f32[4,16,64]{2,1,0:T(8,128)S(1)}, f32[4,16,64]{2,1,0:T(8,128)}, u32[]{:S(2)}) copy-start(f32[4,16,64]{2,1,0:T(8,128)} %param.21) | copy-start | bytes 49156
Sparse Core Ops, SparseCore 0:
  120.6 21.2 all-gather.1
